TPU v7x, 32 devices: a whole 2x2x4 slice. The times are simulated.
32 devices in a mesh: dp: 4 (over y, x), fsdp: 8 (over z, core).
Axes of the slice: x: 2, y: 2, z: 4, core: 2. Of those that a mesh axis runs over, the one named last changes fastest.
Arguments:
- scenes_in: bfloat16 [32, 256, 1024], P(('dp', 'fsdp')), may hold values from -6 to 6
- scene_lengths: int32 [32], P(('dp', 'fsdp')), may hold values from 128 to 256, as said below
- cotangent: bfloat16 [32, 256, 1024], P(('dp', 'fsdp')), may hold values from -6 to 6
- qkv_weight: bfloat16 [1024, 3072], P('fsdp'), may hold values from -0.1875 to 0.1875
- out_weight: bfloat16 [1024, 1024], P('fsdp'), may hold values from -0.75 to 0.75
- up_weight: bfloat16 [1024, 4096], P('fsdp'), may hold values from -0.1875 to 0.1875
- down_weight: bfloat16 [4096, 1024], P('fsdp'), may hold values from -0.125 to 0.125
- gain_one: bfloat16 [1024], P('fsdp'), may hold values from 0.5 to 1.5
- bias_one: bfloat16 [1024], P('fsdp'), may hold values from -2 to 2
- gain_two: bfloat16 [1024], P('fsdp'), may hold values from 0.5 to 1.5
- bias_two: bfloat16 [1024], P('fsdp'), may hold values from -2 to 2
Outputs:
- layer_out: bfloat16 [32, 256, 1024], P(('dp', 'fsdp'))
- input_grad: bfloat16 [32, 256, 1024], P(('dp', 'fsdp'))
- qkv_grad: float32 [1024, 3072], P('fsdp')
- out_grad: float32 [1024, 1024], P('fsdp')
- up_grad: float32 [1024, 4096], P('fsdp')
- down_grad: float32 [4096, 1024], P('fsdp')
- gain_one_grad: float32 [1024], P('fsdp')
- bias_one_grad: float32 [1024], P('fsdp')
- gain_two_grad: float32 [1024], P('fsdp')
- bias_two_grad: float32 [1024], P('fsdp')
Inputs may be any that keep to these rules, and one draw needn't show every extreme that they name: `scene_lengths`: each length is a multiple of 128; some scene has exactly 256 tokens.
All inputs are finite; a program needn't handle non-finite values.
Results may differ from a plain program's by a relative error of at most 0.017.
Values may be sent and summed in bfloat16 or wider, within the bound.
A program may use at most 192 MiB of HBM per device.

v0:
```python
import math
import jax
import jax.numpy as jnp
from jax import lax
from jax.sharding import PartitionSpec as P

D = 1024
HEADS = 16
HEAD_DIM = 64
epsilon = 1e-05


def norm_rows(values_in):
    row_mean = jnp.mean(values_in, axis=-1, keepdims=True)
    centered = values_in - row_mean
    variance = jnp.mean(centered * centered, axis=-1, keepdims=True)
    inverse = lax.rsqrt(variance + epsilon)
    return (centered * inverse, inverse)


def norm_back(grad_normed, normed, inverse):
    first_mean = jnp.mean(grad_normed, axis=-1, keepdims=True)
    second_mean = jnp.mean(grad_normed * normed, axis=-1, keepdims=True)
    return inverse * (grad_normed - first_mean - normed * second_mean)


def inner_rows(left, right):
    return lax.dot_general(
        left, right, (((0,), (0,)), ((), ())), preferred_element_type=jnp.float32
    )


def outer_cols(left, right):
    return lax.dot_general(
        left, right, (((1,), (1,)), ((), ())), preferred_element_type=jnp.float32
    )


def forward_pass(inputs, key_valid, params):
    qkv_weight, out_weight, up_weight, down_weight, gain_one, bias_one, gain_two, bias_two = params
    seq_len = inputs.shape[0]
    normed_one, inverse_one = norm_rows(inputs)
    hidden_one = (normed_one * gain_one.astype(jnp.float32) + bias_one.astype(jnp.float32)).astype(
        jnp.bfloat16
    )
    qkv_low = jnp.dot(hidden_one, qkv_weight, preferred_element_type=jnp.float32).astype(
        jnp.bfloat16
    )
    split_view = qkv_low.reshape(seq_len, 3, HEADS, HEAD_DIM)
    queries = split_view[:, 0]
    keys_all = split_view[:, 1]
    values_all = split_view[:, 2]
    scale_factor = 1.0 / math.sqrt(HEAD_DIM)
    scores = (
        jnp.einsum("qhd,khd->hqk", queries, keys_all, preferred_element_type=jnp.float32)
        * scale_factor
    )
    masked = jnp.where(key_valid[None, None, :], scores, -1e30)
    highest = jnp.max(masked, axis=-1, keepdims=True)
    expont = jnp.exp(masked - highest)
    probs = expont / jnp.sum(expont, axis=-1, keepdims=True)
    probs_low = probs.astype(jnp.bfloat16)
    attended = jnp.einsum("hqk,khd->qhd", probs_low, values_all, preferred_element_type=jnp.float32)
    attn_low = attended.reshape(seq_len, D).astype(jnp.bfloat16)
    resid_one = inputs + jnp.dot(attn_low, out_weight, preferred_element_type=jnp.float32)
    normed_two, inverse_two = norm_rows(resid_one)
    hidden_two = (normed_two * gain_two.astype(jnp.float32) + bias_two.astype(jnp.float32)).astype(
        jnp.bfloat16
    )
    hidden_pre = jnp.dot(hidden_two, up_weight, preferred_element_type=jnp.float32)
    activated = jax.nn.gelu(hidden_pre, approximate=False).astype(jnp.bfloat16)
    result = resid_one + jnp.dot(activated, down_weight, preferred_element_type=jnp.float32)
    return (
        result,
        normed_one,
        inverse_one,
        hidden_one,
        queries,
        keys_all,
        values_all,
        probs,
        probs_low,
        attn_low,
        normed_two,
        inverse_two,
        hidden_two,
        hidden_pre,
        activated,
    )


def mlp_back(grad_out, saved, params):
    up_weight, down_weight, gain_two = (params[2], params[3], params[6])
    normed_two, inverse_two, hidden_two, hidden_pre, activated = (
        saved[10],
        saved[11],
        saved[12],
        saved[13],
        saved[14],
    )
    grad_low = grad_out.astype(jnp.bfloat16)
    down_grad = inner_rows(activated, grad_low)
    grad_act = outer_cols(grad_low, down_weight)
    cumul = 0.5 * (1.0 + lax.erf(hidden_pre * (1.0 / math.sqrt(2.0))))
    density = jnp.exp(-0.5 * hidden_pre * hidden_pre) * (1.0 / math.sqrt(2.0 * math.pi))
    grad_pre = (grad_act * (cumul + hidden_pre * density)).astype(jnp.bfloat16)
    up_grad = inner_rows(hidden_two, grad_pre)
    grad_hidden = outer_cols(grad_pre, up_weight)
    gain_two_grad = jnp.sum(grad_hidden * normed_two, axis=0)
    bias_two_grad = jnp.sum(grad_hidden, axis=0)
    grad_resid = grad_out + norm_back(
        grad_hidden * gain_two.astype(jnp.float32), normed_two, inverse_two
    )
    return (grad_resid, up_grad, down_grad, gain_two_grad, bias_two_grad)


def attn_back(grad_resid, saved, params):
    qkv_weight, out_weight, gain_one = (params[0], params[1], params[4])
    normed_one, inverse_one, hidden_one = (saved[1], saved[2], saved[3])
    queries, keys_all, values_all, probs, probs_low, attn_low = (
        saved[4],
        saved[5],
        saved[6],
        saved[7],
        saved[8],
        saved[9],
    )
    seq_len = grad_resid.shape[0]
    scale_factor = 1.0 / math.sqrt(HEAD_DIM)
    resid_low = grad_resid.astype(jnp.bfloat16)
    out_grad = inner_rows(attn_low, resid_low)
    grad_attn = (
        outer_cols(resid_low, out_weight).astype(jnp.bfloat16).reshape(seq_len, HEADS, HEAD_DIM)
    )
    grad_probs = jnp.einsum(
        "qhd,khd->hqk", grad_attn, values_all, preferred_element_type=jnp.float32
    )
    row_dot = jnp.sum(probs * grad_probs, axis=-1, keepdims=True)
    grad_scores = (probs * (grad_probs - row_dot)).astype(jnp.bfloat16)
    grad_values = jnp.einsum(
        "hqk,qhd->khd", probs_low, grad_attn, preferred_element_type=jnp.float32
    )
    grad_queries = (
        jnp.einsum("hqk,khd->qhd", grad_scores, keys_all, preferred_element_type=jnp.float32)
        * scale_factor
    )
    grad_keys = (
        jnp.einsum("hqk,qhd->khd", grad_scores, queries, preferred_element_type=jnp.float32)
        * scale_factor
    )
    grad_qkv = (
        jnp.stack([grad_queries, grad_keys, grad_values], axis=1)
        .reshape(seq_len, 3 * D)
        .astype(jnp.bfloat16)
    )
    qkv_grad = inner_rows(hidden_one, grad_qkv)
    grad_hidden = outer_cols(grad_qkv, qkv_weight)
    gain_one_grad = jnp.sum(grad_hidden * normed_one, axis=0)
    bias_one_grad = jnp.sum(grad_hidden, axis=0)
    input_grad = grad_resid + norm_back(
        grad_hidden * gain_one.astype(jnp.float32), normed_one, inverse_one
    )
    return (input_grad, qkv_grad, out_grad, gain_one_grad, bias_one_grad)


def on_device(
    scenes_in,
    scene_lengths,
    cotangent,
    qkv_weight,
    out_weight,
    up_weight,
    down_weight,
    gain_one,
    bias_one,
    gain_two,
    bias_two,
):
    params = (
        lax.all_gather(qkv_weight, "fsdp", axis=0, tiled=True),
        lax.all_gather(out_weight, "fsdp", axis=0, tiled=True),
        lax.all_gather(up_weight, "fsdp", axis=0, tiled=True),
        lax.all_gather(down_weight, "fsdp", axis=0, tiled=True),
        lax.all_gather(gain_one, "fsdp", axis=0, tiled=True),
        lax.all_gather(bias_one, "fsdp", axis=0, tiled=True),
        lax.all_gather(gain_two, "fsdp", axis=0, tiled=True),
        lax.all_gather(bias_two, "fsdp", axis=0, tiled=True),
    )
    inputs = scenes_in[0].astype(jnp.float32)
    seq_len = inputs.shape[0]
    positions = jnp.arange(seq_len, dtype=jnp.int32)
    key_valid = positions < scene_lengths[0]
    row_mask = key_valid.astype(jnp.float32)[:, None]
    saved = forward_pass(inputs, key_valid, params)
    layer_out = (saved[0] * row_mask).astype(jnp.bfloat16)[None]
    grad_out = cotangent[0].astype(jnp.float32) * row_mask
    params_back = (
        lax.all_gather(qkv_weight, "fsdp", axis=0, tiled=True),
        lax.all_gather(out_weight, "fsdp", axis=0, tiled=True),
        lax.all_gather(up_weight, "fsdp", axis=0, tiled=True),
        lax.all_gather(down_weight, "fsdp", axis=0, tiled=True),
        lax.all_gather(gain_one, "fsdp", axis=0, tiled=True),
        lax.all_gather(bias_one, "fsdp", axis=0, tiled=True),
        lax.all_gather(gain_two, "fsdp", axis=0, tiled=True),
        lax.all_gather(bias_two, "fsdp", axis=0, tiled=True),
    )
    saved_back = forward_pass(inputs, key_valid, params_back)
    grad_resid, up_grad, down_grad, gain_two_grad, bias_two_grad = mlp_back(
        grad_out, saved_back, params_back
    )
    input_grad, qkv_grad, out_grad, gain_one_grad, bias_one_grad = attn_back(
        grad_resid, saved_back, params_back
    )
    shares = (
        lax.psum_scatter(qkv_grad, "fsdp", scatter_dimension=0, tiled=True),
        lax.psum_scatter(out_grad, "fsdp", scatter_dimension=0, tiled=True),
        lax.psum_scatter(up_grad, "fsdp", scatter_dimension=0, tiled=True),
        lax.psum_scatter(down_grad, "fsdp", scatter_dimension=0, tiled=True),
        lax.psum_scatter(gain_one_grad, "fsdp", scatter_dimension=0, tiled=True),
        lax.psum_scatter(bias_one_grad, "fsdp", scatter_dimension=0, tiled=True),
        lax.psum_scatter(gain_two_grad, "fsdp", scatter_dimension=0, tiled=True),
        lax.psum_scatter(bias_two_grad, "fsdp", scatter_dimension=0, tiled=True),
    )
    summed = (
        lax.psum(shares[0].astype(jnp.bfloat16), "dp").astype(jnp.float32),
        lax.psum(shares[1].astype(jnp.bfloat16), "dp").astype(jnp.float32),
        lax.psum(shares[2].astype(jnp.bfloat16), "dp").astype(jnp.float32),
        lax.psum(shares[3].astype(jnp.bfloat16), "dp").astype(jnp.float32),
        lax.psum(shares[4].astype(jnp.bfloat16), "dp").astype(jnp.float32),
        lax.psum(shares[5].astype(jnp.bfloat16), "dp").astype(jnp.float32),
        lax.psum(shares[6].astype(jnp.bfloat16), "dp").astype(jnp.float32),
        lax.psum(shares[7].astype(jnp.bfloat16), "dp").astype(jnp.float32),
    )
    qkv_total, out_total, up_total, down_total = (summed[0], summed[1], summed[2], summed[3])
    gain_one_total, bias_one_total, gain_two_total, bias_two_total = (
        summed[4],
        summed[5],
        summed[6],
        summed[7],
    )
    input_out = input_grad.astype(jnp.bfloat16)[None]
    return (
        layer_out,
        input_out,
        qkv_total,
        out_total,
        up_total,
        down_total,
        gain_one_total,
        bias_one_total,
        gain_two_total,
        bias_two_total,
    )


def solution(mesh):
    placed = (
        P(("dp", "fsdp"), None, None),
        P(("dp", "fsdp")),
        P(("dp", "fsdp"), None, None),
        P("fsdp", None),
        P("fsdp", None),
        P("fsdp", None),
        P("fsdp", None),
        P("fsdp"),
        P("fsdp"),
        P("fsdp"),
        P("fsdp"),
    )
    return jax.shard_map(
        on_device,
        mesh=mesh,
        in_specs=placed,
        out_specs=(
            P(("dp", "fsdp"), None, None),
            P(("dp", "fsdp"), None, None),
            P("fsdp", None),
            P("fsdp", None),
            P("fsdp", None),
            P("fsdp", None),
            P("fsdp"),
            P("fsdp"),
            P("fsdp"),
            P("fsdp"),
        ),
        check_vma=False,
    )
```

profile of v0, /device:TPU:0, one launch (start us, length us, event | category | flops | bytes accessed | tf_op | source)
XLA Modules:
  0.0 905.0 jit_solution(12101224661716060638)
XLA Ops:
  10.0 13.6 %all-gather = bf16[8,1,128]{2,1,0:T(2,128)(2,1)S(1)} all-gather(bf16[1,1,128]{2,1,0:T(2,128)(2,1)} %bitcast.139), channel_id=1, replica_groups=mesh['dp'=4,'fsdp'=8] {'fsdp'}, dimensions={0}, use_global_device_ids=true | all-gather | bytes 2304 | tf_op jit(solution)/shard_map/all_gather | solution.py:184
  23.7 9.3 %all-gather.1 = bf16[8,1,128]{2,1,0:T(2,128)(2,1)S(1)} all-gather(bf16[1,1,128]{2,1,0:T(2,128)(2,1)} %bitcast.140), channel_id=1, replica_groups=mesh['dp'=4,'fsdp'=8] {'fsdp'}, dimensions={0}, use_global_device_ids=true | all-gather | bytes 2304 | tf_op jit(solution)/shard_map/all_gather | solution.py:185
  33.6 11.4 %all-gather.2 = bf16[8,1,128]{2,1,0:T(2,128)(2,1)S(1)} all-gather(bf16[1,1,128]{2,1,0:T(2,128)(2,1)} %bitcast.141), channel_id=1, replica_groups=mesh['dp'=4,'fsdp'=8] {'fsdp'}, dimensions={0}, use_global_device_ids=true | all-gather | bytes 2304 | tf_op jit(solution)/shard_map/all_gather | solution.py:186
  45.0 9.3 %all-gather.3 = bf16[8,1,128]{2,1,0:T(2,128)(2,1)S(1)} all-gather(bf16[1,1,128]{2,1,0:T(2,128)(2,1)} %bitcast.142), channel_id=1, replica_groups=mesh['dp'=4,'fsdp'=8] {'fsdp'}, dimensions={0}, use_global_device_ids=true | all-gather | bytes 2304 | tf_op jit(solution)/shard_map/all_gather | solution.py:187
  56.9 20.2 %all-gather.9.cloned.1.call-done = bf16[1024,3072]{1,0:T(8,128)(2,1)} async-done(((bf16[128,3072]{1,0:T(8,128)(2,1)}), bf16[1024,3072]{1,0:T(8,128)(2,1)}) %all-gather.9.cloned.1.call-update) | async-done | bytes 6291472 | tf_op jit(solution)/shard_map/all_gather | solution.py:180
  77.1 5.8 convolution_convert_fusion
  89.7 16.8 %all-gather.11.cloned.1.call-done = bf16[1024,1024]{1,0:T(8,128)(2,1)} async-done(((bf16[128,1024]{1,0:T(8,128)(2,1)}), bf16[1024,1024]{1,0:T(8,128)(2,1)}) %all-gather.11.cloned.1.call-update) | async-done | bytes 2097168 | tf_op jit(solution)/shard_map/all_gather | solution.py:181
  106.5 2.4 fusion.76
  109.2 80.4 %all-gather.13.cloned.1.call-done = bf16[1024,4096]{1,0:T(8,128)(2,1)} async-done(((bf16[128,4096]{1,0:T(8,128)(2,1)}), bf16[1024,4096]{1,0:T(8,128)(2,1)}) %all-gather.13.cloned.1.call-update) | async-done | bytes 8388624 | tf_op jit(solution)/shard_map/all_gather | solution.py:182
  189.6 15.3 %fusion.4 = (bf16[256,4096]{1,0:T(8,128)(2,1)}, f32[256,4096]{1,0:T(8,128)}) fusion(bf16[1024,4096]{1,0:T(8,128)(2,1)} %all-gather.13.cloned.1.call-done, f32[256,1024]{1,0:T(8,128)S(1)} %get-tuple-element.33, f32[1024]{0:T(1024)S(1)} %bitcast.131, f32[1024]{0:T(1024)S(1)} %bitcast.127, f32[256]{0:T(256)S(1)} %add_rsqrt_fusion, ...), kind=kOutput, calls=%fused_computation.7 | convolution fusion | flops 2216951808 | bytes 15738880 | tf_op jit(solution)/shard_map/dot_general | solution.py:70
  204.8 66.8 %all-gather.15.cloned.1.call-done = bf16[4096,1024]{1,0:T(8,128)(2,1)} async-done(((bf16[512,1024]{1,0:T(8,128)(2,1)}), bf16[4096,1024]{1,0:T(8,128)(2,1)}) %all-gather.15.cloned.1.call-update) | async-done | bytes 8388624 | tf_op jit(solution)/shard_map/all_gather | solution.py:183
  271.6 6.8 fusion.1
  278.6 2.7 multiply_reduce_fusion.1
  281.8 2.8 fusion.64
  288.0 3.8 multiply_reduce_fusion
  296.9 6.5 fusion.50
  303.8 9.9 %fusion.73 = f32[1024,4096]{1,0:T(8,128)} fusion(bf16[256,4096]{1,0:T(8,128)(2,1)} %copy-done.10, f32[256,1024]{1,0:T(8,128)S(1)} %get-tuple-element.33, f32[1024]{0:T(1024)S(1)} %bitcast.132, f32[1024]{0:T(1024)S(1)} %bitcast.130, f32[256]{0:T(256)S(1)} %add_rsqrt_fusion, f32[256]{0:T(256)S(1)} %broadcast_multiply_fusion.4), kind=kOutput, calls=%fused_computation.121 | convolution fusion | flops 2148794368 | bytes 19933184 | tf_op jit(solution)/shard_map/dot_general | solution.py:28
  314.7 9.8 %fusion.67 = f32[4096,1024]{1,0:T(8,128)} fusion(bf16[256,4096]{1,0:T(8,128)(2,1)} %get-tuple-element.34, bf16[1,256,1024]{2,1,0:T(8,128)(2,1)S(1)} %copy-done.7, f32[256]{0:T(256)S(1)} %fusion.72), kind=kOutput, calls=%fused_computation.104 | convolution fusion | flops 2148270080 | bytes 19399680 | tf_op jit(solution)/shard_map/dot_general | solution.py:28
  324.6 8.6 reduce-scatter.7.cloned.1.call-done
  334.9 128.0 %reduce-scatter.5.cloned.1.call-done = f32[128,3072]{1,0:T(8,128)} async-done(((f32[1024,3072]{1,0:T(8,128)}), f32[128,3072]{1,0:T(8,128)}) %reduce-scatter.5.cloned.1.call-update) | async-done | bytes 1572880 | tf_op jit(solution)/shard_map/reduce_scatter | solution.py:215
  465.4 166.6 %reduce-scatter.9.cloned.1.call-done = f32[128,4096]{1,0:T(8,128)} async-done(((f32[1024,4096]{1,0:T(8,128)}), f32[128,4096]{1,0:T(8,128)}) %reduce-scatter.9.cloned.1.call-update) | async-done | bytes 2097168 | tf_op jit(solution)/shard_map/reduce_scatter | solution.py:217
  632.0 2.7 convert_element_type.187
  634.7 166.3 %reduce-scatter.11.cloned.1.call-done = f32[512,1024]{1,0:T(8,128)} async-done(((f32[4096,1024]{1,0:T(8,128)}), f32[512,1024]{1,0:T(8,128)}) %reduce-scatter.11.cloned.1.call-update) | async-done | bytes 2097168 | tf_op jit(solution)/shard_map/reduce_scatter | solution.py:218
  801.0 2.7 convert_element_type.189
  805.0 6.3 fusion.39
  811.2 25.9 %all-reduce.4 = (bf16[1024]{0:T(1024)(128)(2,1)S(1)}, bf16[1024]{0:T(1024)(128)(2,1)S(1)}, bf16[1024]{0:T(1024)(128)(2,1)S(1)}, bf16[1024]{0:T(1024)(128)(2,1)S(1)}) all-reduce(f32[1024]{0:T(1024)S(1)} %get-tuple-element.12, f32[1024]{0:T(1024)S(1)} %get-tuple-element.17, ...), channel_id=6, replica_groups=mesh['dp'=4,'fsdp'=8] {'fsdp'}, use_global_device_ids=true, to_apply=%region_20.21.clone | all-reduce | flops 4096 | bytes 24576
  837.5 10.2 %all-reduce.5 = (bf16[128]{0:T(256)(128)(2,1)S(1)}, bf16[128]{0:T(256)(128)(2,1)S(1)}, bf16[128]{0:T(256)(128)(2,1)S(1)}, bf16[128]{0:T(256)(128)(2,1)S(1)}) all-reduce(bf16[128]{0:T(256)(128)(2,1)S(1)} %dynamic-slice.15, bf16[128]{0:T(256)(128)(2,1)S(1)} %dynamic-slice.14, ...), channel_id=1, replica_groups=mesh['dp'=4,'fsdp'=8] {'dp'}, use_global_device_ids=true, to_apply=%region_21.22 | all-reduce | flops 512 | bytes 2048 | tf_op jit(solution)/shard_map/psum | solution.py:229
  849.7 2.4 fusion.52
  852.2 7.8 fusion.31
  860.0 30.7 %all-reduce.9.cloned.1.call-done = (bf16[128,3072]{1,0:T(8,128)(2,1)}, bf16[128,1024]{1,0:T(8,128)(2,1)}, bf16[128,4096]{1,0:T(8,128)(2,1)}, bf16[512,1024]{1,0:T(8,128)(2,1)}) async-done(((bf16[128,3072]{1,0:T(8,128)(2,1)}, bf16[128,1024]{1,0:T(8,128)(2,1)}, bf16[128,4096]{1,0:T(8,128)(2,1)}, bf16[512,1024]{1,0:T(8,128)(2,1)}), (bf16[128,3072]{1,0:T(8,128)(2,1)}, bf16[128,1024]{1,0:T(8,128)(2,1)}, ...) | async-done | bytes 3145744 | tf_op jit(solution)/shard_map/psum | solution.py:225
  890.7 2.8 convert_element_type.188
  893.5 2.8 convert_element_type.190
  (91 shorter events, 32.0 us)
Async XLA Ops:
  7.2 69.9 %copy-start = (bf16[1,256,1024]{2,1,0:T(8,128)(2,1)S(1)}, bf16[1,256,1024]{2,1,0:T(8,128)(2,1)}, u32[]{:S(2)}) copy-start(bf16[1,256,1024]{2,1,0:T(8,128)(2,1)} %param.11) | copy-start | bytes 1572868
  7.2 69.9 %all-gather.9.cloned.1.call-start = ((), (), s32[]{:S(2)}) async-start(), calls=%async_computation.4 | async-start | bytes 7077888 | tf_op jit(solution)/shard_map/all_gather | solution.py:180
  7.9 98.6 %all-gather.11.cloned.1.call-start = ((), (), s32[]{:S(2)}) async-start(), calls=%async_computation.5 | async-start | bytes 2359296 | tf_op jit(solution)/shard_map/all_gather | solution.py:181
  8.7 180.9 %all-gather.13.cloned.1.call-start = ((), (), s32[]{:S(2)}) async-start(), calls=%async_computation.6 | async-start | bytes 9437184 | tf_op jit(solution)/shard_map/all_gather | solution.py:182
  9.4 262.2 %all-gather.15.cloned.1.call-start = ((), (), s32[]{:S(2)}) async-start(), calls=%async_computation.7 | async-start | bytes 9437184 | tf_op jit(solution)/shard_map/all_gather | solution.py:183
  10.0 323.2 %reduce-scatter.7.cloned.1.call-start = ((), (), s32[]{:S(2)}) async-start(), calls=%async_computation.9 | async-start | bytes 4718592 | tf_op jit(solution)/shard_map/reduce_scatter | solution.py:216
  84.7 2.5 copy-start.1
  87.2 2.0 copy-start.4
  89.6 115.2 %copy-start.8 = (bf16[16,64,256]{2,1,0:T(8,128)(2,1)}, bf16[16,64,256]{2,1,0:T(8,128)(2,1)S(1)}, u32[]{:S(2)}) copy-start(bf16[16,64,256]{2,1,0:T(8,128)(2,1)S(1)} %convolution_convert_fusion.2) | copy-start | bytes 1572868
  189.6 82.0 %copy-start.6 = (bf16[1,256,1024]{2,1,0:T(8,128)(2,1)S(1)}, bf16[1,256,1024]{2,1,0:T(8,128)(2,1)}, u32[]{:S(2)}) copy-start(bf16[1,256,1024]{2,1,0:T(8,128)(2,1)} %param.13) | copy-start | bytes 1572868
  271.6 7.0 copy-start.14
  278.6 2.7 copy-start.10
  278.6 3.1 copy-start.9
  284.6 178.4 %reduce-scatter.5.cloned.1.call-start = ((), (), s32[]{:S(2)}) async-start(), calls=%async_computation.8 | async-start | bytes 14155776 | tf_op jit(solution)/shard_map/reduce_scatter | solution.py:215
  288.0 4.1 copy-start.5
  292.1 1.4 copy-start.2
  293.5 1.2 copy-start.12
  295.8 1.1 copy-start.3
  303.5 328.5 %reduce-scatter.9.cloned.1.call-start = ((), (), s32[]{:S(2)}) async-start(), calls=%async_computation.10 | async-start | bytes 18874368 | tf_op jit(solution)/shard_map/reduce_scatter | solution.py:217
  313.7 1.0 copy-start.7
  313.7 487.3 %reduce-scatter.11.cloned.1.call-start = ((), (), s32[]{:S(2)}) async-start(), calls=%async_computation.11 | async-start | bytes 18874368 | tf_op jit(solution)/shard_map/reduce_scatter | solution.py:218
  324.6 566.1 %all-reduce.9.cloned.1.call-start = ((), (), s32[]{:S(2)}) async-start(), calls=%async_computation.12 | async-start | bytes 6291456 | tf_op jit(solution)/shard_map/psum | solution.py:225
  465.4 338.4 %copy-start.15 = (u32[32]{0:T(128)S(1)}, u32[32]{0:T(128)}, u32[]{:S(2)}) copy-start(u32[32]{0:T(128)} %constant.89) | copy-start | bytes 388
  890.7 5.6 copy-start.11
  890.7 6.9 copy-start.13
Sparse Core Ops, SparseCore 0:
  9.6 67.4 all-gather.8
  78.7 27.7 all-gather.10
  108.1 81.4 all-gather.12
  191.0 80.5 all-gather.14
  284.7 48.4 reduce-scatter.6
  335.3 127.5 reduce-scatter.4
  465.3 166.6 reduce-scatter.8
  634.3 166.6 reduce-scatter.10
  804.9 85.7 all-reduce.8
where the time goes:
time: 906 us; the launch traced here: 905 us
  waiting for transfers between devices  687 us (76%)
  matrix products  85.6 us (9%)
  blocking collectives  79.8 us (9%)
  other arithmetic  27.9 us (3%)
  between operations  15.4 us (2%)
    reduce_scatter x1, waiting for transfers between devices, on_device(): lax.psum_scatter(up_grad, 'fsdp', scatter_dimension=0, tiled=True)  167 us
    reduce_scatter x1, waiting for transfers between devices, on_device(): lax.psum_scatter(down_grad, 'fsdp', scatter_dimension=0, tiled=True)  166 us
    reduce_scatter x1, waiting for transfers between devices, on_device(): lax.psum_scatter(qkv_grad, 'fsdp', scatter_dimension=0, tiled=True)  128 us
    all_gather x1, waiting for transfers between devices, on_device(): lax.all_gather(up_weight, 'fsdp', axis=0, tiled=True)  80.4 us
    all_gather x1, waiting for transfers between devices, on_device(): lax.all_gather(down_weight, 'fsdp', axis=0, tiled=True)  66.8 us
    psum x1, waiting for transfers between devices, on_device(): lax.psum(shares[0].astype(jnp.bfloat16), 'dp').astype(jnp.float32)  30.7 us
    dot_general x4, matrix products, inner_rows(): lax.dot_general(left, right, (((0,), (0,)), ((), ())), preferred_element_...  29.1 us
    unnamed x1, blocking collectives  25.9 us
  transfers between devices with their start and end apart: 9, of which 9 were waited for; matrix products, arithmetic and copies ran while one was open for 10% of the time, Pallas kernels for 0%

commit v1 on v0

--- a/solution.py
+++ b/solution.py
@@ -8,6 +8,11 @@
 HEADS = 16
 HEAD_DIM = 64
 epsilon = 1e-05
+
+
+def store_knots(block_in):
+    b_now = lax.all_gather(block_in, "dp").sum(axis=0)
+    return b_now
 
 
 def norm_rows(values_in):
@@ -222,7 +227,7 @@
         lax.psum_scatter(bias_two_grad, "fsdp", scatter_dimension=0, tiled=True),
     )
     summed = (
-        lax.psum(shares[0].astype(jnp.bfloat16), "dp").astype(jnp.float32),
+        store_knots(shares[0].astype(jnp.bfloat16)).astype(jnp.float32),
         lax.psum(shares[1].astype(jnp.bfloat16), "dp").astype(jnp.float32),
         lax.psum(shares[2].astype(jnp.bfloat16), "dp").astype(jnp.float32),
         lax.psum(shares[3].astype(jnp.bfloat16), "dp").astype(jnp.float32),

time: 906 us -> 951 us (1.050)
  waiting for transfers between devices: 687 us -> 730 us
    reduce_scatter x1, waiting for transfers between devices: 8.55 us -> 48.1 us  [on_device(): lax.psum_scatter(out_grad, 'fsdp', scatter_dimension=0, tiled=True)]
    psum x1, waiting for transfers between devices: 30.7 us -> 59.2 us  [on_device(): lax.psum(shares[1].astype(jnp.bfloat16), 'dp').astype(jnp.float32)]
    reduce_scatter x1, waiting for transfers between devices: 128 us -> 102 us  [on_device(): lax.psum_scatter(qkv_grad, 'fsdp', scatter_dimension=0, tiled=True)]
  transfers between devices with their start and end apart: 9 -> 10, of which waited for: 9 -> 9; matrix products, arithmetic and copies ran while one was open for 10% -> 9% of each run, Pallas kernels for 0% -> 0%
where the time goes in v1:
time: 951 us; the launch traced here: 950 us
  waiting for transfers between devices  730 us (77%)
  matrix products  84.2 us (9%)
  blocking collectives  79.6 us (8%)
  other arithmetic  30.4 us (3%)
  between operations  15.7 us (2%)
  local copies, waits for them, and re-layouts  9.68 us (1%)
    reduce_scatter x1, waiting for transfers between devices, on_device(): lax.psum_scatter(up_grad, 'fsdp', scatter_dimension=0, tiled=True)  167 us
    reduce_scatter x1, waiting for transfers between devices, on_device(): lax.psum_scatter(down_grad, 'fsdp', scatter_dimension=0, tiled=True)  166 us
    reduce_scatter x1, waiting for transfers between devices, on_device(): lax.psum_scatter(qkv_grad, 'fsdp', scatter_dimension=0, tiled=True)  102 us
    all_gather x1, waiting for transfers between devices, on_device(): lax.all_gather(up_weight, 'fsdp', axis=0, tiled=True)  80.4 us
    all_gather x1, waiting for transfers between devices, on_device(): lax.all_gather(down_weight, 'fsdp', axis=0, tiled=True)  66.8 us
    psum x1, waiting for transfers between devices, on_device(): lax.psum(shares[1].astype(jnp.bfloat16), 'dp').astype(jnp.float32)  59.2 us
    reduce_scatter x1, waiting for transfers between devices, on_device(): lax.psum_scatter(out_grad, 'fsdp', scatter_dimension=0, tiled=True)  48.1 us
    dot_general x4, matrix products, inner_rows(): lax.dot_general(left, right, (((0,), (0,)), ((), ())), preferred_element_...  29.4 us
  transfers between devices with their start and end apart: 10, of which 9 were waited for; matrix products, arithmetic and copies ran while one was open for 9% of the time, Pallas kernels for 0%

profile of v1, /device:TPU:0, one launch (start us, length us, event | category | flops | bytes accessed | tf_op | source)
XLA Modules:
  0.0 950.5 jit_solution(619713570947713279)
XLA Ops:
  10.0 13.6 %all-gather.1 = bf16[8,1,128]{2,1,0:T(2,128)(2,1)S(1)} all-gather(bf16[1,1,128]{2,1,0:T(2,128)(2,1)} %bitcast.141), channel_id=1, replica_groups=mesh['dp'=4,'fsdp'=8] {'fsdp'}, dimensions={0}, use_global_device_ids=true | all-gather | bytes 2304 | tf_op jit(solution)/shard_map/all_gather | solution.py:189
  23.7 9.3 all-gather.2
  33.6 11.4 %all-gather.3 = bf16[8,1,128]{2,1,0:T(2,128)(2,1)S(1)} all-gather(bf16[1,1,128]{2,1,0:T(2,128)(2,1)} %bitcast.143), channel_id=1, replica_groups=mesh['dp'=4,'fsdp'=8] {'fsdp'}, dimensions={0}, use_global_device_ids=true | all-gather | bytes 2304 | tf_op jit(solution)/shard_map/all_gather | solution.py:191
  45.0 9.3 all-gather.4
  56.9 20.2 %all-gather.11.cloned.1.call-done = bf16[1024,3072]{1,0:T(8,128)(2,1)} async-done(((bf16[128,3072]{1,0:T(8,128)(2,1)}), bf16[1024,3072]{1,0:T(8,128)(2,1)}) %all-gather.11.cloned.1.call-update) | async-done | bytes 6291472 | tf_op jit(solution)/shard_map/all_gather | solution.py:185
  77.1 5.8 convolution_convert_fusion
  89.7 16.8 %all-gather.13.cloned.1.call-done = bf16[1024,1024]{1,0:T(8,128)(2,1)} async-done(((bf16[128,1024]{1,0:T(8,128)(2,1)}), bf16[1024,1024]{1,0:T(8,128)(2,1)}) %all-gather.13.cloned.1.call-update) | async-done | bytes 2097168 | tf_op jit(solution)/shard_map/all_gather | solution.py:186
  109.2 80.4 %all-gather.15.cloned.1.call-done = bf16[1024,4096]{1,0:T(8,128)(2,1)} async-done(((bf16[128,4096]{1,0:T(8,128)(2,1)}), bf16[1024,4096]{1,0:T(8,128)(2,1)}) %all-gather.15.cloned.1.call-update) | async-done | bytes 8388624 | tf_op jit(solution)/shard_map/all_gather | solution.py:187
  189.6 15.3 %fusion.4 = (bf16[256,4096]{1,0:T(8,128)(2,1)}, f32[256,4096]{1,0:T(8,128)}) fusion(bf16[1024,4096]{1,0:T(8,128)(2,1)} %all-gather.15.cloned.1.call-done, f32[256,1024]{1,0:T(8,128)S(1)} %get-tuple-element.32, f32[1024]{0:T(1024)S(1)} %bitcast.133, f32[1024]{0:T(1024)S(1)} %bitcast.129, f32[256]{0:T(256)S(1)} %add_rsqrt_fusion, ...), kind=kOutput, calls=%fused_computation.7 | convolution fusion | flops 2216951808 | bytes 15738880 | tf_op jit(solution)/shard_map/dot_general | solution.py:75
  204.8 66.8 %all-gather.17.cloned.1.call-done = bf16[4096,1024]{1,0:T(8,128)(2,1)} async-done(((bf16[512,1024]{1,0:T(8,128)(2,1)}), bf16[4096,1024]{1,0:T(8,128)(2,1)}) %all-gather.17.cloned.1.call-update) | async-done | bytes 8388624 | tf_op jit(solution)/shard_map/all_gather | solution.py:188
  271.6 6.8 fusion.1
  278.6 2.7 multiply_reduce_fusion.1
  283.5 3.5 multiply_reduce_fusion
  292.0 6.5 fusion.50
  299.6 2.8 fusion.64
  302.8 10.3 %fusion.73 = f32[1024,4096]{1,0:T(8,128)} fusion(bf16[256,4096]{1,0:T(8,128)(2,1)} %copy-done.11, f32[256,1024]{1,0:T(8,128)S(1)} %get-tuple-element.32, f32[1024]{0:T(1024)S(1)} %bitcast.134, f32[1024]{0:T(1024)S(1)} %bitcast.132, f32[256]{0:T(256)S(1)} %add_rsqrt_fusion, f32[256]{0:T(256)S(1)} %broadcast_multiply_fusion.4), kind=kOutput, calls=%fused_computation.121 | convolution fusion | flops 2148794368 | bytes 19933184 | tf_op jit(solution)/shard_map/dot_general | solution.py:33
  314.1 9.7 %fusion.67 = f32[4096,1024]{1,0:T(8,128)} fusion(bf16[256,4096]{1,0:T(8,128)(2,1)} %get-tuple-element.33, bf16[1,256,1024]{2,1,0:T(8,128)(2,1)S(1)} %copy-done.8, f32[256]{0:T(256)S(1)} %fusion.72), kind=kOutput, calls=%fused_computation.104 | convolution fusion | flops 2148270080 | bytes 19399680 | tf_op jit(solution)/shard_map/dot_general | solution.py:33
  323.9 102.5 %reduce-scatter.5.cloned.1.call-done = f32[128,3072]{1,0:T(8,128)} async-done(((f32[1024,3072]{1,0:T(8,128)}), f32[128,3072]{1,0:T(8,128)}) %reduce-scatter.5.cloned.1.call-update) | async-done | bytes 1572880 | tf_op jit(solution)/shard_map/reduce_scatter | solution.py:220
  428.8 48.1 %reduce-scatter.7.cloned.1.call-done = f32[128,1024]{1,0:T(8,128)} async-done(((f32[1024,1024]{1,0:T(8,128)}), f32[128,1024]{1,0:T(8,128)}) %reduce-scatter.7.cloned.1.call-update) | async-done | bytes 524304 | tf_op jit(solution)/shard_map/reduce_scatter | solution.py:221
  478.7 167.3 %reduce-scatter.9.cloned.1.call-done = f32[128,4096]{1,0:T(8,128)} async-done(((f32[1024,4096]{1,0:T(8,128)}), f32[128,4096]{1,0:T(8,128)}) %reduce-scatter.9.cloned.1.call-update) | async-done | bytes 2097168 | tf_op jit(solution)/shard_map/reduce_scatter | solution.py:222
  646.0 2.7 convert_element_type.189
  648.7 166.3 %reduce-scatter.11.cloned.1.call-done = f32[512,1024]{1,0:T(8,128)} async-done(((f32[4096,1024]{1,0:T(8,128)}), f32[512,1024]{1,0:T(8,128)}) %reduce-scatter.11.cloned.1.call-update) | async-done | bytes 2097168 | tf_op jit(solution)/shard_map/reduce_scatter | solution.py:223
  815.0 2.7 convert_element_type.191
  819.0 6.4 fusion.39
  825.4 25.9 %all-reduce.4 = (bf16[1024]{0:T(1024)(128)(2,1)S(1)}, bf16[1024]{0:T(1024)(128)(2,1)S(1)}, bf16[1024]{0:T(1024)(128)(2,1)S(1)}, bf16[1024]{0:T(1024)(128)(2,1)S(1)}) all-reduce(f32[1024]{0:T(1024)S(1)} %get-tuple-element.12, f32[1024]{0:T(1024)S(1)} %get-tuple-element.17, ...), channel_id=7, replica_groups=mesh['dp'=4,'fsdp'=8] {'fsdp'}, use_global_device_ids=true, to_apply=%region_20.21.clone | all-reduce | flops 4096 | bytes 24576
  851.7 10.0 %all-reduce.5 = (bf16[128]{0:T(256)(128)(2,1)S(1)}, bf16[128]{0:T(256)(128)(2,1)S(1)}, bf16[128]{0:T(256)(128)(2,1)S(1)}, bf16[128]{0:T(256)(128)(2,1)S(1)}) all-reduce(bf16[128]{0:T(256)(128)(2,1)S(1)} %dynamic-slice.15, bf16[128]{0:T(256)(128)(2,1)S(1)} %dynamic-slice.14, ...), channel_id=1, replica_groups=mesh['dp'=4,'fsdp'=8] {'dp'}, use_global_device_ids=true, to_apply=%region_21.22 | all-reduce | flops 512 | bytes 2048 | tf_op jit(solution)/shard_map/psum | solution.py:234
  863.8 2.4 fusion.52
  866.2 7.9 fusion.31
  874.1 2.6 reduce_sum.168
  878.0 59.2 %all-reduce.9.cloned.1.call-done = (bf16[128,1024]{1,0:T(8,128)(2,1)}, bf16[128,4096]{1,0:T(8,128)(2,1)}, bf16[512,1024]{1,0:T(8,128)(2,1)}) async-done(((bf16[128,1024]{1,0:T(8,128)(2,1)}, bf16[128,4096]{1,0:T(8,128)(2,1)}, bf16[512,1024]{1,0:T(8,128)(2,1)}), (bf16[128,1024]{1,0:T(8,128)(2,1)}, bf16[128,4096]{1,0:T(8,128)(2,1)}, bf16[512,1024]{1,0:T(8,128)(2,1)})) %all-reduce.9.cloned.1.call-update) | async-done | bytes 2359312 | tf_op jit(solution)/shard_map/psum | solution.py:231
  937.2 2.8 convert_element_type.190
  940.0 2.8 convert_element_type.192
  (95 shorter events, 33.9 us)
Async XLA Ops:
  7.2 69.9 %copy-start = (bf16[1,256,1024]{2,1,0:T(8,128)(2,1)S(1)}, bf16[1,256,1024]{2,1,0:T(8,128)(2,1)}, u32[]{:S(2)}) copy-start(bf16[1,256,1024]{2,1,0:T(8,128)(2,1)} %param.11) | copy-start | bytes 1572868
  7.2 69.9 %all-gather.11.cloned.1.call-start = ((), (), s32[]{:S(2)}) async-start(), calls=%async_computation.4 | async-start | bytes 7077888 | tf_op jit(solution)/shard_map/all_gather | solution.py:185
  7.9 98.6 %all-gather.13.cloned.1.call-start = ((), (), s32[]{:S(2)}) async-start(), calls=%async_computation.5 | async-start | bytes 2359296 | tf_op jit(solution)/shard_map/all_gather | solution.py:186
  8.7 180.9 %all-gather.15.cloned.1.call-start = ((), (), s32[]{:S(2)}) async-start(), calls=%async_computation.6 | async-start | bytes 9437184 | tf_op jit(solution)/shard_map/all_gather | solution.py:187
  9.4 262.2 %all-gather.17.cloned.1.call-start = ((), (), s32[]{:S(2)}) async-start(), calls=%async_computation.7 | async-start | bytes 9437184 | tf_op jit(solution)/shard_map/all_gather | solution.py:188
  10.0 416.4 %reduce-scatter.5.cloned.1.call-start = ((), (), s32[]{:S(2)}) async-start(), calls=%async_computation.8 | async-start | bytes 14155776 | tf_op jit(solution)/shard_map/reduce_scatter | solution.py:220
  84.7 2.5 copy-start.1
  87.2 2.0 copy-start.5
  89.6 115.2 %copy-start.9 = (bf16[16,64,256]{2,1,0:T(8,128)(2,1)}, bf16[16,64,256]{2,1,0:T(8,128)(2,1)S(1)}, u32[]{:S(2)}) copy-start(bf16[16,64,256]{2,1,0:T(8,128)(2,1)S(1)} %convolution_convert_fusion.2) | copy-start | bytes 1572868
  189.6 82.0 %copy-start.7 = (bf16[1,256,1024]{2,1,0:T(8,128)(2,1)S(1)}, bf16[1,256,1024]{2,1,0:T(8,128)(2,1)}, u32[]{:S(2)}) copy-start(bf16[1,256,1024]{2,1,0:T(8,128)(2,1)} %param.13) | copy-start | bytes 1572868
  271.6 7.0 copy-start.14
  278.6 2.7 copy-start.11
  278.6 3.1 copy-start.3
  283.5 3.7 copy-start.6
  287.3 1.4 copy-start.2
  288.7 1.2 copy-start.12
  290.9 1.1 copy-start.4
  298.6 1.0 copy-start.10
  298.6 178.3 %reduce-scatter.7.cloned.1.call-start = ((), (), s32[]{:S(2)}) async-start(), calls=%async_computation.9 | async-start | bytes 4718592 | tf_op jit(solution)/shard_map/reduce_scatter | solution.py:221
  302.5 343.5 %reduce-scatter.9.cloned.1.call-start = ((), (), s32[]{:S(2)}) async-start(), calls=%async_computation.10 | async-start | bytes 18874368 | tf_op jit(solution)/shard_map/reduce_scatter | solution.py:222
  313.0 1.0 copy-start.8
  313.1 501.9 %reduce-scatter.11.cloned.1.call-start = ((), (), s32[]{:S(2)}) async-start(), calls=%async_computation.11 | async-start | bytes 18874368 | tf_op jit(solution)/shard_map/reduce_scatter | solution.py:223
  323.9 550.3 %all-gather.19.cloned.1.call-start = ((), (), s32[]{:S(2)}) async-start(), calls=%async_computation.12 | async-start | bytes 3932160 | tf_op jit(solution)/shard_map/all_gather | solution.py:14
  428.8 508.4 %all-reduce.9.cloned.1.call-start = ((), (), s32[]{:S(2)}) async-start(), calls=%async_computation.13 | async-start | bytes 4718592 | tf_op jit(solution)/shard_map/psum | solution.py:231
  478.7 339.0 %copy-start.15 = (u32[32]{0:T(128)S(1)}, u32[32]{0:T(128)}, u32[]{:S(2)}) copy-start(u32[32]{0:T(128)} %constant.91) | copy-start | bytes 388
  937.2 5.6 copy-start.13
Sparse Core Ops, SparseCore 0:
  9.6 67.4 all-gather.10
  78.7 27.7 all-gather.12
  108.1 81.4 all-gather.14
  191.0 80.5 all-gather.16
  298.7 127.6 reduce-scatter.4
  428.5 48.3 reduce-scatter.6
  479.3 166.6 reduce-scatter.8
  648.3 166.6 reduce-scatter.10
  816.8 42.4 all-gather.18
  863.2 73.9 all-reduce.8
